TPU v7x, 128 devices: a whole 4x4x4 slice. The times are simulated.
128 devices in a mesh: rep: 16 (over x, y), exp: 8 (over z, core).
Axes of the slice: x: 4, y: 4, z: 4, core: 2. Of those that a mesh axis runs over, the one named last changes fastest.
Arguments:
- hidden: bfloat16 [16384, 4096], P(('rep', 'exp')), may hold values from -6 to 6
- parents: int32 [16384], P(('rep', 'exp')), may hold values from 0 to 1023
- routes: int32 [16384, 8], P(('rep', 'exp')), may hold values from 0 to 127, all different within a row; in each aligned block of 128 rows (0 to 127, 128 to 255, ...) at most 10 rows name the same one
- gates: float32 [16384, 8], P(('rep', 'exp')), may hold values from 0.05 to 1
- counts: int32 [128], P(('rep', 'exp')), may hold values from 64 to 128, as said below
- norm_gain: float32 [4096], replicated, may hold values from 0.1 to 1.9
- w_gate: bfloat16 [128, 4096, 768], P(('rep', 'exp')), may hold values from -0.09375 to 0.09375
- w_up: bfloat16 [128, 4096, 768], P(('rep', 'exp')), may hold values from -0.09375 to 0.09375
- w_down: bfloat16 [128, 768, 4096], P(('rep', 'exp')), may hold values from -0.21875 to 0.21875
Outputs:
- mixed: bfloat16 [16384, 4096], P(('rep', 'exp'))
Inputs may be any that keep to these rules, and one draw needn't show every extreme that they name: `routes`: in the rows of one device no expert is named more than 10 times. `counts`: some device has all of its rows live.
All inputs are finite; a program needn't handle non-finite values.
Results may differ from a plain program's by a relative error of at most 0.0071.
Values may be sent and summed in bfloat16 or wider, within the bound.
A program may use at most 128 MiB of HBM per device.

v0:
```python
import jax
import jax.numpy as jnp
from jax import lax
from jax.sharding import PartitionSpec as P


def run_expert(arrived, w_gate, w_up, w_down):
    gate_val = jnp.dot(arrived, w_gate[0], preferred_element_type=jnp.float32)
    up_val = jnp.dot(arrived, w_up[0], preferred_element_type=jnp.float32)
    act = (jax.nn.silu(gate_val) * up_val).astype(jnp.bfloat16)
    return jnp.dot(act, w_down[0], preferred_element_type=jnp.float32).astype(jnp.bfloat16)


def shards(hidden, parents, routes, gates, counts, norm_gain, w_gate, w_up, w_down):
    rows = hidden.shape[0]
    width = hidden.shape[1]
    top = routes.shape[1]
    n_rep = lax.axis_size("rep")
    n_exp = lax.axis_size("exp")
    n_dev = n_rep * n_exp
    cap = rows * top // n_dev + 2
    column = lax.axis_index("exp")
    micro = rows * n_exp
    per_expert = cap * n_exp
    slots = n_rep * per_expert
    live = jnp.arange(rows, dtype=jnp.int32) < counts[0]
    weights = gates / jnp.sum(gates, axis=1, keepdims=True) * live[:, None].astype(jnp.float32)
    flat = routes.reshape(-1)
    live_slot = jnp.repeat(live, top)
    onehot = (
        (flat[:, None] == jnp.arange(n_dev, dtype=jnp.int32)[None, :]) & live_slot[:, None]
    ).astype(jnp.int32)
    before = jnp.cumsum(onehot, axis=0) - onehot
    rank = jnp.sum(before * onehot, axis=1)
    code = jnp.where(live_slot, flat, -1)
    ints = jnp.concatenate(
        [code.reshape(rows, top), rank.reshape(rows, top), parents[:, None]], axis=1
    )
    group = lax.all_gather(hidden, "exp", axis=0, tiled=True)
    ints_all = lax.all_gather(ints, "exp", axis=0, tiled=True)
    w_all = lax.all_gather(weights, "exp", axis=0, tiled=True)
    code_all = ints_all[:, :top]
    rank_all = ints_all[:, top : 2 * top]
    parent_all = ints_all[:, 2 * top]
    mine = (code_all >= 0) & (code_all % n_exp == column)
    owner = (jnp.arange(micro, dtype=jnp.int32) // rows)[:, None]
    dest = code_all // n_exp * per_expert + owner * cap + rank_all
    dest = jnp.where(mine, dest, slots).reshape(-1)
    row_id = jnp.broadcast_to(jnp.arange(micro, dtype=jnp.int32)[:, None], (micro, top)).reshape(-1)
    src_row = jnp.zeros((slots,), jnp.int32).at[dest].set(row_id, mode="drop")
    filled = jnp.zeros((slots,), jnp.bool_).at[dest].set(True, mode="drop")
    slot_w = jnp.zeros((slots,), jnp.float32).at[dest].set(w_all.reshape(-1), mode="drop")
    picked = jnp.take(group, jnp.take(parent_all, src_row), axis=0).astype(jnp.float32)
    scale = lax.rsqrt(jnp.mean(picked * picked, axis=1, keepdims=True) + 1e-06)
    normed = (picked * scale * norm_gain).astype(jnp.bfloat16)
    outgoing = jnp.where(filled[:, None], normed, jnp.zeros((), jnp.bfloat16))
    arrived = lax.all_to_all(outgoing, "rep", split_axis=0, concat_axis=0, tiled=True)
    results = run_expert(arrived, w_gate, w_up, w_down)
    returned = lax.all_to_all(results, "rep", split_axis=0, concat_axis=0, tiled=True)
    contrib = slot_w[:, None] * returned.astype(jnp.float32)
    target = jnp.where(filled, src_row, micro)
    partial = jnp.zeros((micro, width), jnp.float32).at[target].add(contrib, mode="drop")
    mixed = lax.psum_scatter(partial.astype(jnp.bfloat16), "exp", scatter_dimension=0, tiled=True)
    return mixed


def solution(mesh):
    placed = (
        P(("rep", "exp"), None),
        P(("rep", "exp")),
        P(("rep", "exp"), None),
        P(("rep", "exp"), None),
        P(("rep", "exp")),
        P(),
        P(("rep", "exp"), None, None),
        P(("rep", "exp"), None, None),
        P(("rep", "exp"), None, None),
    )
    return jax.shard_map(
        shards, mesh=mesh, in_specs=placed, out_specs=P(("rep", "exp"), None), check_vma=False
    )
```

profile of v0, /device:TPU:1, one launch (start us, length us, event | category | flops | bytes accessed | tf_op | source)
XLA Modules:
  0.0 590.4 jit_solution(2126128571061677138)
XLA Ops:
  6.5 0.0 all-gather.2.cloned.1.call-start
  6.5 0.7 all-gather.2.cloned.1.call-update
  7.3 0.8 copy.28
  8.0 0.1 eq.37
  8.1 0.1 eq.33
  8.9 0.1 broadcast_in_dim.94.clone
  9.0 0.1 and.55
  9.1 0.1 copy.31
  9.2 0.3 fusion.17
  9.7 0.1 copy.32
  9.8 0.5 fusion.16
  10.3 0.1 reshape.149
  10.4 0.7 broadcast_select_fusion
  11.1 0.7 pad_add_fusion
  11.8 15.3 %all_gather.9 = s32[1024,17]{0,1:T(8,128)S(1)} all-gather(s32[128,17]{0,1:T(8,128)S(1)} %pad_add_fusion), channel_id=1, replica_groups=mesh['rep'=16,'exp'=8] {'exp'}, dimensions={0}, use_global_device_ids=true | all-gather | bytes 78336 | tf_op jit(solution)/shard_map/all_gather | solution.py:40
  27.1 0.2 copy.34
  27.3 0.3 reshape.150
  27.7 34.6 %scatter_custom_fusion = pred[1280]{0:T(1024)(128)(4,1)S(1)} fusion(s32[8192]{0:T(1024)S(1)} %bitcast.48, pred[8192]{0:T(1024)(128)(4,1)S(1)} %broadcast.149, pred[]{:T(512)} %constant.90.clone.1), kind=kCustom, calls=%fused_computation.72 | custom fusion | bytes 1281 | tf_op jit(solution)/shard_map/scatter | solution.py:51
  62.3 0.1 broadcast_in_dim.105
  62.4 0.3 reshape.182
  62.7 30.9 %scatter_custom_fusion.1 = s32[1280]{0:T(1024)S(1)} fusion(s32[8192]{0:T(1024)S(1)} %bitcast.49, s32[8192]{0:T(1024)S(1)} %reshape.182, s32[]{:T(128)} %constant.93.clone.1), kind=kCustom, calls=%fused_computation.69 | custom fusion | bytes 5124 | tf_op jit(solution)/shard_map/scatter | solution.py:50
  93.6 5.0 gather_fusion
  98.6 0.1 broadcast_in_dim.109
  98.7 0.0 all-gather.2.cloned.1.call-done
  98.7 23.2 %gather_fusion.1 = bf16[1280,4096]{1,0:T(8,128)(2,1)} fusion(bf16[1024,4096]{1,0:T(8,128)(2,1)} %all-gather.2.cloned.1.call-done, s32[2048]{0:T(1024)S(1)} %pad_clamp_fusion), kind=kCustom, calls=%fused_computation.1 | custom fusion | bytes 20976640 | tf_op jit(solution)/shard_map/jit(_take)/gather | solution.py:53
  121.9 0.0 copy-start
  121.9 6.9 %multiply_reduce_fusion = f32[1280]{0:T(1024)S(1)} fusion(bf16[1280,4096]{1,0:T(8,128)(2,1)} %gather_fusion.1, pred[1280]{0:T(1024)(128)(4,1)S(1)} %get-tuple-element.5), kind=kLoop, calls=%fused_computation.9 | loop fusion | flops 20970240 | bytes 10492160 | tf_op jit(solution)/shard_map/reduce_sum | solution.py:54
  128.8 0.1 rsqrt.12
  128.9 0.0 copy-done
  128.9 9.0 %fusion.1 = bf16[16,80,4096]{2,1,0:T(8,128)(2,1)S(1)} fusion(f32[4096]{0:T(1024)S(1)} %copy-done, f32[16,80]{1,0:T(8,128)S(1)} %rsqrt.12, bf16[16,80,4096]{2,1,0:T(8,128)(2,1)} %bitcast.44, pred[16,80]{1,0:T(8,128)(4,1)S(1)} %broadcast_in_dim.109, pred[16,80]{1,0:T(8,128)(4,1)S(1)} %broadcast_in_dim.105), kind=kLoop, calls=%fused_computation.11 | loop fusion | flops 31457280 | bytes 20995584 | tf_op jit(solution)/shard_map/jit(_where)/select_n | solution.py:56
  138.0 0.0 slice-start
  138.0 0.0 slice-start.2
  138.0 123.9 %all_to_all.18 = bf16[16,80,4096]{2,1,0:T(8,128)(2,1)S(1)} all-to-all(bf16[16,80,4096]{2,1,0:T(8,128)(2,1)S(1)} %fusion.1), channel_id=1, replica_groups=mesh['rep'=16,'exp'=8] {'rep'}, dimensions={0} | all-to-all | bytes 20971520 | tf_op jit(solution)/shard_map/all_to_all | solution.py:57
  261.9 0.0 slice-start.1
  261.9 0.0 slice-start.3
  261.9 11.8 %fusion.7 = f32[1280,768]{1,0:T(8,128)} fusion(bf16[1280,4096]{1,0:T(8,128)(2,1)S(1)} %bitcast.46, bf16[1,4096,768]{2,1,0:T(8,128)(2,1)} %param.15), kind=kOutput, calls=%fused_computation.17 | convolution fusion | flops 8053063680 | bytes 20709376 | tf_op jit(solution)/shard_map/dot_general | solution.py:8
  273.7 0.0 slice-done
  273.7 0.0 slice-done.1
  273.7 10.3 %fusion.12 = bf16[1280,768]{1,0:T(8,128)(2,1)S(1)} fusion(bf16[1280,4096]{1,0:T(8,128)(2,1)S(1)} %bitcast.47, bf16[1,4096,768]{2,1,0:T(8,128)(2,1)S(1)} %bitcast.53, f32[1280,768]{1,0:T(8,128)} %fusion.7), kind=kOutput, calls=%fused_computation.20 | convolution fusion | flops 8058961920 | bytes 22675456 | tf_op jit(solution)/shard_map/dot_general | solution.py:9
  284.0 0.0 slice-done.2
  284.0 0.0 slice-done.3
  284.1 10.7 %convolution_convert_fusion = bf16[1280,4096]{1,0:T(8,128)(2,1)} fusion(bf16[1280,768]{1,0:T(8,128)(2,1)S(1)} %fusion.12, bf16[1,768,4096]{2,1,0:T(8,128)(2,1)S(1)} %bitcast.55), kind=kOutput, calls=%fused_computation.10 | convolution fusion | flops 8058306560 | bytes 18743296 | tf_op jit(solution)/shard_map/dot_general | solution.py:11
  294.7 0.0 copy-start.1
  294.7 5.0 all-to-all-start.1
  299.7 0.0 reduce-scatter.2.cloned.1.call-start
  299.8 0.0 copy-done.1
  299.8 14.9 %all_gather.10 = f32[1024,8]{0,1:T(8,128)S(1)} all-gather(f32[128,8]{0,1:T(8,128)S(1)} %divide_multiply_fusion), channel_id=1, replica_groups=mesh['rep'=16,'exp'=8] {'exp'}, dimensions={0}, use_global_device_ids=true | all-gather | bytes 36864 | tf_op jit(solution)/shard_map/all_gather | solution.py:41
  314.7 0.2 copy.35
  314.9 0.3 reshape.190
  315.1 30.4 %scatter_custom_fusion.2 = f32[1280]{0:T(1024)S(1)} fusion(s32[8192]{0:T(1024)S(1)} %bitcast.50, f32[8192]{0:T(1024)S(1)} %reshape.190, f32[]{:T(128)} %constant.89.clone.1), kind=kCustom, calls=%fused_computation.67 | custom fusion | bytes 5124 | tf_op jit(solution)/shard_map/scatter | solution.py:52
  345.6 126.3 %all-to-all-done.1 = bf16[16,80,4096]{2,1,0:T(8,128)(2,1)} async-done(((bf16[16,80,4096]{2,1,0:T(8,128)(2,1)}), bf16[16,80,4096]{2,1,0:T(8,128)(2,1)}, u32[]{:S(2)}, u32[]{:S(2)}) %all-to-all-start.1) | async-done | bytes 10485792 | tf_op jit(solution)/shard_map/all_to_all | solution.py:59
  471.9 42.9 %scatter_custom_fusion.3 = f32[1024,4096]{1,0:T(8,128)} fusion(s32[1280]{0:T(1024)S(1)} %get-tuple-element.8, bf16[1280,4096]{1,0:T(8,128)(2,1)} %bitcast.16, f32[1280]{0:T(1024)S(1)} %scatter_custom_fusion.2, f32[]{:T(128)} %constant.89.clone.1), kind=kCustom, calls=%fused_computation.7 | custom fusion | flops 15728640 | bytes 27271172 | tf_op jit(solution)/shard_map/scatter-add | solution.py:62
  514.8 9.0 %convert_element_type.50 = bf16[1024,4096]{1,0:T(8,128)(2,1)} convert(f32[1024,4096]{1,0:T(8,128)} %scatter_custom_fusion.3) | non-fusion elementwise | flops 4194304 | bytes 25165824 | tf_op jit(solution)/shard_map/convert_element_type | solution.py:63
  523.8 0.0 reduce-scatter.2.cloned.1.call-update
  523.8 59.5 %reduce-scatter.2.cloned.1.call-done = bf16[128,4096]{1,0:T(8,128)(2,1)} async-done(((bf16[1024,4096]{1,0:T(8,128)(2,1)}), bf16[128,4096]{1,0:T(8,128)(2,1)}) %reduce-scatter.2.cloned.1.call-update) | async-done | bytes 1048592 | tf_op jit(solution)/shard_map/reduce_scatter | solution.py:63
  (24 shorter events, 0.3 us)
Async XLA Ops:
  6.5 92.2 %all-gather.2.cloned.1.call-start = ((), (), s32[]{:S(2)}) async-start(), calls=%async_computation.3 | async-start | bytes 9437184 | tf_op jit(solution)/shard_map/all_gather | solution.py:39
  121.9 7.0 %copy-start = (f32[4096]{0:T(1024)S(1)}, f32[4096]{0:T(1024)}, u32[]{:S(2)}) copy-start(f32[4096]{0:T(1024)} %param.14) | copy-start | bytes 49156
  138.0 135.8 %slice-start = ((s8[6291456]{0:T(1024)(128)(4,1)}), s8[4194304]{0:T(1024)(128)(4,1)S(1)}, s32[]{:S(2)}) async-start(s8[6291456]{0:T(1024)(128)(4,1)} %bitcast.52), calls=%async_computation.5 | async-start | bytes 8388608
  138.0 146.1 %slice-start.2 = ((s8[6291456]{0:T(1024)(128)(4,1)}), s8[4194304]{0:T(1024)(128)(4,1)S(1)}, s32[]{:S(2)}) async-start(s8[6291456]{0:T(1024)(128)(4,1)} %bitcast.54), calls=%async_computation.7 | async-start | bytes 8388608
  261.9 11.8 %slice-start.1 = ((s8[6291456]{0:T(1024)(128)(4,1)}), s8[2097152]{0:T(1024)(128)(4,1)S(1)}, s32[]{:S(2)}) async-start(s8[6291456]{0:T(1024)(128)(4,1)} %bitcast.52), calls=%async_computation.6 | async-start | bytes 4194304
  261.9 22.2 %slice-start.3 = ((s8[6291456]{0:T(1024)(128)(4,1)}), s8[2097152]{0:T(1024)(128)(4,1)S(1)}, s32[]{:S(2)}) async-start(s8[6291456]{0:T(1024)(128)(4,1)} %bitcast.54), calls=%async_computation.8 | async-start | bytes 4194304
  294.7 5.0 copy-start.1
  294.7 177.1 %all-to-all-start.1 = ((bf16[16,80,4096]{2,1,0:T(8,128)(2,1)}), bf16[16,80,4096]{2,1,0:T(8,128)(2,1)}, u32[]{:S(2)}, u32[]{:S(2)}) async-start(bf16[16,80,4096]{2,1,0:T(8,128)(2,1)} %bitcast.45), calls=%async_computation.1 | async-start | bytes 20971520 | tf_op jit(solution)/shard_map/all_to_all | solution.py:59
  299.7 283.6 %reduce-scatter.2.cloned.1.call-start = ((), (), s32[]{:S(2)}) async-start(), calls=%async_computation.4 | async-start | bytes 9437184 | tf_op jit(solution)/shard_map/reduce_scatter | solution.py:63
Sparse Core Ops, SparseCore 0:
  9.1 53.5 all-gather.1
  523.9 59.3 reduce-scatter.1
where the time goes:
time: 597 us; the launch traced here: 590 us
  waiting for transfers between devices  187 us (31%)
  blocking collectives  154 us (26%)
  local copies, waits for them, and re-layouts  127 us (21%)
  other arithmetic  70.3 us (12%)
  matrix products  32.8 us (5%)
  between operations  14.6 us (2%)
    all_to_all x1, waiting for transfers between devices, shards(): lax.all_to_all(results, 'rep', split_axis=0, concat_axis=0, tiled=True)  126 us
    all_to_all x1, blocking collectives, shards(): lax.all_to_all(outgoing, 'rep', split_axis=0, concat_axis=0, tiled=True)  124 us
    reduce_scatter x1, waiting for transfers between devices, shards(): lax.psum_scatter(partial.astype(jnp.bfloat16), 'exp', scatter_dimension=0...  59.5 us
    scatter-add x1, other arithmetic, shards(): jnp.zeros((micro, width), jnp.float32).at[target].add(contrib, mode='drop')  42.9 us
    scatter x1, local copies, waits for them, and re-layouts, shards(): filled = jnp.zeros((slots,), jnp.bool_).at[dest].set(True, mode='drop')  34.6 us
    scatter x1, local copies, waits for them, and re-layouts, shards(): src_row = jnp.zeros((slots,), jnp.int32).at[dest].set(row_id, mode='drop')  30.9 us
    scatter x1, local copies, waits for them, and re-layouts, shards(): jnp.zeros((slots,), jnp.float32).at[dest]  30.4 us
    gather x1, local copies, waits for them, and re-layouts, shards(): jnp.take(group, jnp.take(parent_all, src_row), axis=0).astype(jnp.float32)  23.2 us
  transfers between devices with their start and end apart: 3, of which 2 were waited for; matrix products, arithmetic and copies ran while one was open for 18% of the time, Pallas kernels for 0%

commit v1 on v0

--- a/solution.py
+++ b/solution.py
@@ -2,6 +2,22 @@
 import jax.numpy as jnp
 from jax import lax
 from jax.sharding import PartitionSpec as P
+
+
+def swapped_with_each(x, axis, split, join):
+    ways, here = (lax.axis_size(axis), lax.axis_index(axis))
+    width = x.shape[split] // ways
+    shape = list(x.shape)
+    shape[split] = width
+    height = shape[join]
+    shape[join] = height * ways
+    full = jnp.zeros(shape, x.dtype)
+    for mask in range(ways):
+        part = lax.dynamic_slice_in_dim(x, (here ^ mask) * width, width, axis=split)
+        if mask:
+            part = lax.ppermute(part, axis, [(d, d ^ mask) for d in range(ways)])
+        full = lax.dynamic_update_slice_in_dim(full, part, (here ^ mask) * height, axis=join)
+    return full
 
 
 def run_expert(arrived, w_gate, w_up, w_down):
@@ -56,7 +72,7 @@
     outgoing = jnp.where(filled[:, None], normed, jnp.zeros((), jnp.bfloat16))
     arrived = lax.all_to_all(outgoing, "rep", split_axis=0, concat_axis=0, tiled=True)
     results = run_expert(arrived, w_gate, w_up, w_down)
-    returned = lax.all_to_all(results, "rep", split_axis=0, concat_axis=0, tiled=True)
+    returned = swapped_with_each(results, "rep", 0, 0)
     contrib = slot_w[:, None] * returned.astype(jnp.float32)
     target = jnp.where(filled, src_row, micro)
     partial = jnp.zeros((micro, width), jnp.float32).at[target].add(contrib, mode="drop")

time: 597 us -> 732 us (1.23)
  waiting for transfers between devices: 187 us -> 360 us
  blocking collectives: 154 us -> 29.9 us
  local copies, waits for them, and re-layouts: 127 us -> 159 us
  starting transfers between devices: 5.02 us -> 35 us
  other arithmetic: 70.3 us -> 91.1 us
    ppermute x0 -> x15, waiting for transfers between devices: none -> 130 us  [swapped_with_each(): part = lax.ppermute(part, axis, [(d, d ^ mask) for d in range(ways)])]
    all_to_all x1 -> x0, blocking collectives: 124 us -> none  [shards(): lax.all_to_all(outgoing, 'rep', split_axis=0, concat_axis=0, tiled=True)]
    all_to_all x1, waiting for transfers between devices: 126 us -> 179 us  [shards(): lax.all_to_all(outgoing, 'rep', split_axis=0, concat_axis=0, tiled=True)]
    ppermute x0 -> x15, starting transfers between devices: none -> 27.8 us  [swapped_with_each(): part = lax.ppermute(part, axis, [(d, d ^ mask) for d in range(ways)])]
    dynamic_update_slice x0 -> x15, local copies, waits for them, and re-layouts: none -> 15.6 us  [swapped_with_each(): lax.dynamic_update_slice_in_dim(full, part, (here ^ mask) * height, axis=...]
    convert_element_type x0 -> x1, other arithmetic: none -> 13.9 us  [shards(): contrib = slot_w[:, None] * returned.astype(jnp.float32)]
    reduce_scatter x1, waiting for transfers between devices: 59.5 us -> 50 us  [shards(): lax.psum_scatter(partial.astype(jnp.bfloat16), 'exp', scatter_dimension=0...]
    mul x0 -> x1, local copies, waits for them, and re-layouts: none -> 8.38 us  [shards(): contrib = slot_w[:, None] * returned.astype(jnp.float32)]
  transfers between devices with their start and end apart: 3 -> 18, of which waited for: 2 -> 11; matrix products, arithmetic and copies ran while one was open for 18% -> 17% of each run, Pallas kernels for 0% -> 0%
where the time goes in v1:
time: 732 us; the launch traced here: 726 us
  waiting for transfers between devices  360 us (49%)
  local copies, waits for them, and re-layouts  159 us (22%)
  other arithmetic  91.1 us (12%)
  matrix products  35.2 us (5%)
  starting transfers between devices  35 us (5%)
  blocking collectives  29.9 us (4%)
  between operations  14.7 us (2%)
    all_to_all x1, waiting for transfers between devices, shards(): lax.all_to_all(outgoing, 'rep', split_axis=0, concat_axis=0, tiled=True)  179 us
    ppermute x15, waiting for transfers between devices, swapped_with_each(): part = lax.ppermute(part, axis, [(d, d ^ mask) for d in range(ways)])  130 us
    reduce_scatter x1, waiting for transfers between devices, shards(): lax.psum_scatter(partial.astype(jnp.bfloat16), 'exp', scatter_dimension=0...  50 us
    scatter-add x1, other arithmetic, shards(): jnp.zeros((micro, width), jnp.float32).at[target].add(contrib, mode='drop')  46.9 us
    scatter x1, local copies, waits for them, and re-layouts, shards(): filled = jnp.zeros((slots,), jnp.bool_).at[dest].set(True, mode='drop')  34.6 us
    scatter x1, local copies, waits for them, and re-layouts, shards(): src_row = jnp.zeros((slots,), jnp.int32).at[dest].set(row_id, mode='drop')  30.6 us
    scatter x1, local copies, waits for them, and re-layouts, shards(): jnp.zeros((slots,), jnp.float32).at[dest]  30.4 us
    ppermute x15, starting transfers between devices, swapped_with_each(): part = lax.ppermute(part, axis, [(d, d ^ mask) for d in range(ways)])  27.8 us
  transfers between devices with their start and end apart: 18, of which 11 were waited for; matrix products, arithmetic and copies ran while one was open for 17% of the time, Pallas kernels for 0%

profile of v1, /device:TPU:1, one launch (start us, length us, event | category | flops | bytes accessed | tf_op | source)
XLA Modules:
  0.0 725.6 jit_solution(3093043576242978220)
XLA Ops:
  6.5 0.7 all-gather.2.cloned.1.call-update
  7.3 0.8 copy.28
  9.2 0.3 fusion.17
  9.8 0.5 fusion.16
  10.4 0.7 broadcast_select_fusion
  11.1 0.7 pad_add_fusion
  11.8 15.3 %all_gather.9 = s32[1024,17]{0,1:T(8,128)S(1)} all-gather(s32[128,17]{0,1:T(8,128)S(1)} %pad_add_fusion), channel_id=1, replica_groups=mesh['rep'=16,'exp'=8] {'exp'}, dimensions={0}, use_global_device_ids=true | all-gather | bytes 78336 | tf_op jit(solution)/shard_map/all_gather | solution.py:56
  27.3 0.3 reshape.146
  27.7 34.6 %scatter_custom_fusion = pred[1280]{0:T(1024)(128)(4,1)S(1)} fusion(s32[8192]{0:T(1024)S(1)} %bitcast.42, pred[8192]{0:T(1024)(128)(4,1)S(1)} %broadcast.155, pred[]{:T(512)} %constant.56.clone.1), kind=kCustom, calls=%fused_computation.102 | custom fusion | bytes 1281 | tf_op jit(solution)/shard_map/scatter | solution.py:67
  62.7 30.6 %scatter_custom_fusion.1 = s32[1280]{0:T(1024)S(1)} fusion(s32[8192]{0:T(1024)S(1)} %bitcast.43, s32[8192]{0:T(1024)S(1)} %reshape.177, s32[]{:T(128)} %constant.59.clone.1), kind=kCustom, calls=%fused_computation.99 | custom fusion | bytes 5124 | tf_op jit(solution)/shard_map/scatter | solution.py:66
  93.3 5.0 gather_fusion
  98.4 23.2 %gather_fusion.1 = bf16[1280,4096]{1,0:T(8,128)(2,1)} fusion(bf16[1024,4096]{1,0:T(8,128)(2,1)} %all-gather.2.cloned.1.call-done, s32[2048]{0:T(1024)S(1)} %pad_clamp_fusion), kind=kCustom, calls=%fused_computation.1 | custom fusion | bytes 20976640 | tf_op jit(solution)/shard_map/jit(_take)/gather | solution.py:69
  121.6 6.9 multiply_reduce_fusion
  128.6 11.9 %fusion.2 = bf16[16,80,4096]{2,1,0:T(8,128)(2,1)} fusion(f32[4096]{0:T(1024)S(1)} %copy-done.2, f32[16,80]{1,0:T(8,128)S(1)} %rsqrt.12, bf16[16,80,4096]{2,1,0:T(8,128)(2,1)} %bitcast.41, pred[16,80]{1,0:T(8,128)(4,1)S(1)} %broadcast_in_dim.113, pred[16,80]{1,0:T(8,128)(4,1)S(1)} %broadcast_in_dim.109), kind=kLoop, calls=%fused_computation.11 | loop fusion | flops 31457280 | bytes 20995584 | tf_op jit(solution)/shard_map/jit(_where)/select_n | solution.py:72
  140.5 6.9 all-to-all-start
  147.8 179.2 %all-to-all-done = bf16[16,80,4096]{2,1,0:T(8,128)(2,1)} async-done(((bf16[16,80,4096]{2,1,0:T(8,128)(2,1)}), bf16[16,80,4096]{2,1,0:T(8,128)(2,1)}, u32[]{:S(2)}, u32[]{:S(2)}) %all-to-all-start) | async-done | bytes 10485792 | tf_op jit(solution)/shard_map/all_to_all | solution.py:73
  327.0 12.3 %fusion.7 = f32[1280,768]{1,0:T(8,128)S(1)} fusion(bf16[1280,4096]{1,0:T(8,128)(2,1)} %bitcast.9, bf16[1,4096,768]{2,1,0:T(8,128)(2,1)} %param.15), kind=kOutput, calls=%fused_computation.16 | convolution fusion | flops 8053063680 | bytes 20709376 | tf_op jit(solution)/shard_map/dot_general | solution.py:24
  339.3 11.2 %fusion.12 = bf16[1280,768]{1,0:T(8,128)(2,1)S(1)} fusion(bf16[1280,4096]{1,0:T(8,128)(2,1)} %bitcast.9, bf16[1,4096,768]{2,1,0:T(8,128)(2,1)S(1)} %bitcast.47, f32[1280,768]{1,0:T(8,128)S(1)} %fusion.7), kind=kOutput, calls=%fused_computation.19 | convolution fusion | flops 8058961920 | bytes 22675456 | tf_op jit(solution)/shard_map/dot_general | solution.py:25
  350.5 11.7 %convolution_convert_fusion = bf16[1280,4096]{1,0:T(8,128)(2,1)S(1)} fusion(bf16[1280,768]{1,0:T(8,128)(2,1)S(1)} %fusion.12, bf16[1,768,4096]{2,1,0:T(8,128)(2,1)} %param.17), kind=kOutput, calls=%fused_computation.10 | convolution fusion | flops 8058306560 | bytes 18743296 | tf_op jit(solution)/shard_map/dot_general | solution.py:27
  362.3 5.3 broadcast_in_dim.108
  367.5 3.4 constant_dynamic-slice_fusion
  370.9 3.5 collective-permute-start
  374.6 14.6 %all_gather.10 = f32[1024,8]{0,1:T(8,128)S(1)} all-gather(f32[128,8]{0,1:T(8,128)S(1)} %divide_multiply_fusion), channel_id=1, replica_groups=mesh['rep'=16,'exp'=8] {'exp'}, dimensions={0}, use_global_device_ids=true | all-gather | bytes 36864 | tf_op jit(solution)/shard_map/all_gather | solution.py:57
  389.6 30.4 %scatter_custom_fusion.2 = f32[1280]{0:T(1024)S(1)} fusion(s32[8192]{0:T(1024)S(1)} %bitcast.44, f32[8192]{0:T(1024)S(1)} %reshape.185, f32[]{:T(128)} %constant.53.clone.1), kind=kCustom, calls=%fused_computation.97 | custom fusion | bytes 5124 | tf_op jit(solution)/shard_map/scatter | solution.py:68
  420.2 3.6 collective-permute-start.13
  423.8 1.5 collective-permute-start.12
  425.3 2.3 collective-permute-start.2
  427.6 2.0 constant_dynamic-update-slice_fusion.13
  429.6 1.8 collective-permute-start.3
  431.3 2.0 constant_dynamic-update-slice_fusion.12
  433.3 34.9 %collective-permute-done.2 = bf16[80,4096]{1,0:T(8,128)(2,1)S(1)} collective-permute-done((bf16[80,4096]{1,0:T(8,128)(2,1)}, bf16[80,4096]{1,0:T(8,128)(2,1)S(1)}, u32[]{:S(2)}, u32[]{:S(2)}) %collective-permute-start.2) | collective-permute-done | bytes 655392 | tf_op jit(solution)/shard_map/ppermute | solution.py:18
  468.4 0.9 constant_dynamic-update-slice_fusion.11
  469.3 4.3 collective-permute-start.5
  473.6 0.9 constant_dynamic-update-slice_fusion.10
  474.5 10.7 %collective-permute-done.4 = bf16[80,4096]{1,0:T(8,128)(2,1)S(1)} collective-permute-done((bf16[80,4096]{1,0:T(8,128)(2,1)}, bf16[80,4096]{1,0:T(8,128)(2,1)S(1)}, u32[]{:S(2)}, u32[]{:S(2)}) %collective-permute-start.4) | collective-permute-done | bytes 655392 | tf_op jit(solution)/shard_map/ppermute | solution.py:18
  485.2 2.3 collective-permute-start.6
  487.5 0.9 constant_dynamic-update-slice_fusion.9
  488.3 13.3 %collective-permute-done.5 = bf16[80,4096]{1,0:T(8,128)(2,1)S(1)} collective-permute-done((bf16[80,4096]{1,0:T(8,128)(2,1)}, bf16[80,4096]{1,0:T(8,128)(2,1)S(1)}, u32[]{:S(2)}, u32[]{:S(2)}) %collective-permute-start.5) | collective-permute-done | bytes 655392 | tf_op jit(solution)/shard_map/ppermute | solution.py:18
  501.6 2.2 collective-permute-start.7
  503.9 0.9 constant_dynamic-update-slice_fusion.8
  504.8 10.4 %collective-permute-done.6 = bf16[80,4096]{1,0:T(8,128)(2,1)S(1)} collective-permute-done((bf16[80,4096]{1,0:T(8,128)(2,1)}, bf16[80,4096]{1,0:T(8,128)(2,1)S(1)}, u32[]{:S(2)}, u32[]{:S(2)}) %collective-permute-start.6) | collective-permute-done | bytes 655392 | tf_op jit(solution)/shard_map/ppermute | solution.py:18
  515.3 1.5 collective-permute-start.8
  516.8 0.9 constant_dynamic-update-slice_fusion.7
  517.7 11.6 %collective-permute-done.7 = bf16[80,4096]{1,0:T(8,128)(2,1)S(1)} collective-permute-done((bf16[80,4096]{1,0:T(8,128)(2,1)}, bf16[80,4096]{1,0:T(8,128)(2,1)S(1)}, u32[]{:S(2)}, u32[]{:S(2)}) %collective-permute-start.7) | collective-permute-done | bytes 655392 | tf_op jit(solution)/shard_map/ppermute | solution.py:18
  529.3 1.9 collective-permute-start.9
  531.3 0.9 constant_dynamic-update-slice_fusion.6
  532.2 12.1 %collective-permute-done.8 = bf16[80,4096]{1,0:T(8,128)(2,1)S(1)} collective-permute-done((bf16[80,4096]{1,0:T(8,128)(2,1)}, bf16[80,4096]{1,0:T(8,128)(2,1)S(1)}, u32[]{:S(2)}, u32[]{:S(2)}) %collective-permute-start.8) | collective-permute-done | bytes 655392 | tf_op jit(solution)/shard_map/ppermute | solution.py:18
  544.2 1.1 collective-permute-start.10
  545.3 0.9 constant_dynamic-update-slice_fusion.5
  546.2 12.2 %collective-permute-done.9 = bf16[80,4096]{1,0:T(8,128)(2,1)S(1)} collective-permute-done((bf16[80,4096]{1,0:T(8,128)(2,1)}, bf16[80,4096]{1,0:T(8,128)(2,1)S(1)}, u32[]{:S(2)}, u32[]{:S(2)}) %collective-permute-start.9) | collective-permute-done | bytes 655392 | tf_op jit(solution)/shard_map/ppermute | solution.py:18
  558.4 1.4 collective-permute-start.11
  559.9 0.9 constant_dynamic-update-slice_fusion.4
  560.8 11.6 %collective-permute-done.10 = bf16[80,4096]{1,0:T(8,128)(2,1)S(1)} collective-permute-done((bf16[80,4096]{1,0:T(8,128)(2,1)S(1)}, bf16[80,4096]{1,0:T(8,128)(2,1)S(1)}, u32[]{:S(2)}, u32[]{:S(2)}) %collective-permute-start.10) | collective-permute-done | bytes 655392 | tf_op jit(solution)/shard_map/ppermute | solution.py:18
  572.3 0.9 constant_dynamic-update-slice_fusion.3
  573.2 13.6 %collective-permute-done.11 = bf16[80,4096]{1,0:T(8,128)(2,1)S(1)} collective-permute-done((bf16[80,4096]{1,0:T(8,128)(2,1)S(1)}, bf16[80,4096]{1,0:T(8,128)(2,1)S(1)}, u32[]{:S(2)}, u32[]{:S(2)}) %collective-permute-start.11) | collective-permute-done | bytes 655392 | tf_op jit(solution)/shard_map/ppermute | solution.py:18
  586.8 0.9 constant_dynamic-update-slice_fusion.2
  587.7 0.9 constant_dynamic-update-slice_fusion.1
  588.6 0.9 constant_dynamic-update-slice_fusion
  589.5 0.9 constant_dynamic-update-slice_fusion.14
  590.4 13.9 %convert_element_type.45 = f32[1280,4096]{1,0:T(8,128)} convert(bf16[1280,4096]{1,0:T(8,128)(2,1)} %constant_dynamic-update-slice_fusion.14) | non-fusion elementwise | flops 5242880 | bytes 31457280 | tf_op jit(solution)/shard_map/convert_element_type | solution.py:76
  604.3 8.4 %mul.135 = f32[1280,4096]{1,0:T(8,128)} broadcast(f32[1280]{0:T(1024)S(1)} %scatter_custom_fusion.2), dimensions={0} | broadcast | bytes 20976640 | tf_op jit(solution)/shard_map/mul | solution.py:76
  612.7 46.9 %scatter_custom_fusion.3 = f32[1024,4096]{1,0:T(8,128)} fusion(s32[1280]{0:T(1024)S(1)} %get-tuple-element.24, f32[1280,4096]{1,0:T(8,128)} %mul.135, f32[1280,4096]{1,0:T(8,128)} %convert_element_type.45, f32[]{:T(128)} %constant.53.clone.1), kind=kCustom, calls=%fused_computation.6 | custom fusion | flops 10485760 | bytes 58720260 | tf_op jit(solution)/shard_map/scatter-add | solution.py:78
  659.5 9.0 %convert_element_type.46 = bf16[1024,4096]{1,0:T(8,128)(2,1)} convert(f32[1024,4096]{1,0:T(8,128)} %scatter_custom_fusion.3) | non-fusion elementwise | flops 4194304 | bytes 25165824 | tf_op jit(solution)/shard_map/convert_element_type | solution.py:79
  668.6 50.0 %reduce-scatter.2.cloned.1.call-done = bf16[128,4096]{1,0:T(8,128)(2,1)} async-done(((bf16[1024,4096]{1,0:T(8,128)(2,1)}), bf16[128,4096]{1,0:T(8,128)(2,1)}) %reduce-scatter.2.cloned.1.call-update) | async-done | bytes 1048592 | tf_op jit(solution)/shard_map/reduce_scatter | solution.py:79
  (62 shorter events, 2.8 us)
Async XLA Ops:
  6.5 91.9 %all-gather.2.cloned.1.call-start = ((), (), s32[]{:S(2)}) async-start(), calls=%async_computation.2 | async-start | bytes 9437184 | tf_op jit(solution)/shard_map/all_gather | solution.py:55
  121.6 7.0 copy-start.2
  140.5 198.8 %slice-start = ((s8[6291456]{0:T(1024)(128)(4,1)}), s8[2097152]{0:T(1024)(128)(4,1)S(1)}, s32[]{:S(2)}) async-start(s8[6291456]{0:T(1024)(128)(4,1)} %bitcast.46), calls=%async_computation.4 | async-start | bytes 4194304
  140.5 186.5 %all-to-all-start = ((bf16[16,80,4096]{2,1,0:T(8,128)(2,1)}), bf16[16,80,4096]{2,1,0:T(8,128)(2,1)}, u32[]{:S(2)}, u32[]{:S(2)}) async-start(bf16[16,80,4096]{2,1,0:T(8,128)(2,1)} %fusion.2), calls=%async_computation | async-start | bytes 20971520 | tf_op jit(solution)/shard_map/all_to_all | solution.py:73
  147.4 571.2 %reduce-scatter.2.cloned.1.call-start = ((), (), s32[]{:S(2)}) async-start(), calls=%async_computation.3 | async-start | bytes 9437184 | tf_op jit(solution)/shard_map/reduce_scatter | solution.py:79
  327.0 12.3 %slice-start.1 = ((s8[6291456]{0:T(1024)(128)(4,1)}), s8[4194304]{0:T(1024)(128)(4,1)S(1)}, s32[]{:S(2)}) async-start(s8[6291456]{0:T(1024)(128)(4,1)} %bitcast.46), calls=%async_computation.5 | async-start | bytes 8388608
  367.5 6.9 copy-start.3
  370.9 54.4 %collective-permute-start = (bf16[80,4096]{1,0:T(8,128)(2,1)}, bf16[80,4096]{1,0:T(8,128)(2,1)}, u32[]{:S(2)}, u32[]{:S(2)}) collective-permute-start(bf16[80,4096]{1,0:T(8,128)(2,1)} %get-tuple-element.21), channel_id=1, source_target_pairs={{0,8},{8,0},{16,24},{24,16},{32,40},{40,32},{48,56},{56,48},{64,72... | collective-permute-start | bytes 1966088 | tf_op jit(solution)/shard_map/ppermute | solution.py:18
  374.5 55.1 %collective-permute-start.1 = (bf16[80,4096]{1,0:T(8,128)(2,1)}, bf16[80,4096]{1,0:T(8,128)(2,1)}, u32[]{:S(2)}, u32[]{:S(2)}) collective-permute-start(bf16[80,4096]{1,0:T(8,128)(2,1)} %get-tuple-element.20), channel_id=1, source_target_pairs={{0,16},{8,24},{16,0},{24,8},{32,48},{40,56},{48,32},{56,40},{64,80... | collective-permute-start | bytes 1966088 | tf_op jit(solution)/shard_map/ppermute | solution.py:18
  389.6 168.8 %copy-start = (bf16[80,4096]{1,0:T(8,128)(2,1)S(1)}, bf16[80,4096]{1,0:T(8,128)(2,1)}, u32[]{:S(2)}) copy-start(bf16[80,4096]{1,0:T(8,128)(2,1)} %get-tuple-element.10) | copy-start | bytes 1966084
  420.1 124.1 %copy-start.1 = (bf16[80,4096]{1,0:T(8,128)(2,1)S(1)}, bf16[80,4096]{1,0:T(8,128)(2,1)}, u32[]{:S(2)}) copy-start(bf16[80,4096]{1,0:T(8,128)(2,1)} %get-tuple-element.11) | copy-start | bytes 1966084
  420.1 169.4 %collective-permute-start.14 = (bf16[80,4096]{1,0:T(8,128)(2,1)S(1)}, bf16[80,4096]{1,0:T(8,128)(2,1)S(1)}, u32[]{:S(2)}, u32[]{:S(2)}) collective-permute-start(bf16[80,4096]{1,0:T(8,128)(2,1)S(1)} %get-tuple-element.7), channel_id=1, source_target_pairs={{0,120},{8,112},{16,104},{24,96},{32,88},{40,80},{48,72},{56,64},{... | collective-permute-start | bytes 1966088 | tf_op jit(solution)/shard_map/ppermute | solution.py:18
  420.2 168.4 %collective-permute-start.13 = (bf16[80,4096]{1,0:T(8,128)(2,1)S(1)}, bf16[80,4096]{1,0:T(8,128)(2,1)S(1)}, u32[]{:S(2)}, u32[]{:S(2)}) collective-permute-start(bf16[80,4096]{1,0:T(8,128)(2,1)S(1)} %get-tuple-element.8), channel_id=1, source_target_pairs={{0,112},{8,120},{16,96},{24,104},{32,80},{40,88},{48,64},{56,72},{... | collective-permute-start | bytes 1966088 | tf_op jit(solution)/shard_map/ppermute | solution.py:18
  423.8 163.9 %collective-permute-start.12 = (bf16[80,4096]{1,0:T(8,128)(2,1)S(1)}, bf16[80,4096]{1,0:T(8,128)(2,1)S(1)}, u32[]{:S(2)}, u32[]{:S(2)}) collective-permute-start(bf16[80,4096]{1,0:T(8,128)(2,1)S(1)} %get-tuple-element.9), channel_id=1, source_target_pairs={{0,104},{8,96},{16,120},{24,112},{32,72},{40,64},{48,88},{56,80},{... | collective-permute-start | bytes 1966088 | tf_op jit(solution)/shard_map/ppermute | solution.py:18
  425.3 42.9 %collective-permute-start.2 = (bf16[80,4096]{1,0:T(8,128)(2,1)}, bf16[80,4096]{1,0:T(8,128)(2,1)S(1)}, u32[]{:S(2)}, u32[]{:S(2)}) collective-permute-start(bf16[80,4096]{1,0:T(8,128)(2,1)} %get-tuple-element.19), channel_id=1, source_target_pairs={{0,24},{8,16},{16,8},{24,0},{32,56},{40,48},{48,40},{56,32},{64,88... | collective-permute-start | bytes 1966088 | tf_op jit(solution)/shard_map/ppermute | solution.py:18
  429.6 39.7 %collective-permute-start.3 = (bf16[80,4096]{1,0:T(8,128)(2,1)}, bf16[80,4096]{1,0:T(8,128)(2,1)S(1)}, u32[]{:S(2)}, u32[]{:S(2)}) collective-permute-start(bf16[80,4096]{1,0:T(8,128)(2,1)} %get-tuple-element.18), channel_id=1, source_target_pairs={{0,32},{8,40},{16,48},{24,56},{32,0},{40,8},{48,16},{56,24},{64,96... | collective-permute-start | bytes 1966088 | tf_op jit(solution)/shard_map/ppermute | solution.py:18
  468.2 16.9 %collective-permute-start.4 = (bf16[80,4096]{1,0:T(8,128)(2,1)}, bf16[80,4096]{1,0:T(8,128)(2,1)S(1)}, u32[]{:S(2)}, u32[]{:S(2)}) collective-permute-start(bf16[80,4096]{1,0:T(8,128)(2,1)} %get-tuple-element.17), channel_id=1, source_target_pairs={{0,40},{8,32},{16,56},{24,48},{32,8},{40,0},{48,24},{56,16},{64,10... | collective-permute-start | bytes 1966088 | tf_op jit(solution)/shard_map/ppermute | solution.py:18
  469.3 32.4 %collective-permute-start.5 = (bf16[80,4096]{1,0:T(8,128)(2,1)}, bf16[80,4096]{1,0:T(8,128)(2,1)S(1)}, u32[]{:S(2)}, u32[]{:S(2)}) collective-permute-start(bf16[80,4096]{1,0:T(8,128)(2,1)} %get-tuple-element.16), channel_id=1, source_target_pairs={{0,48},{8,56},{16,32},{24,40},{32,16},{40,24},{48,0},{56,8},{64,11... | collective-permute-start | bytes 1966088 | tf_op jit(solution)/shard_map/ppermute | solution.py:18
  485.2 30.1 %collective-permute-start.6 = (bf16[80,4096]{1,0:T(8,128)(2,1)}, bf16[80,4096]{1,0:T(8,128)(2,1)S(1)}, u32[]{:S(2)}, u32[]{:S(2)}) collective-permute-start(bf16[80,4096]{1,0:T(8,128)(2,1)} %get-tuple-element.15), channel_id=1, source_target_pairs={{0,56},{8,48},{16,40},{24,32},{32,24},{40,16},{48,8},{56,0},{64,12... | collective-permute-start | bytes 1966088 | tf_op jit(solution)/shard_map/ppermute | solution.py:18
  501.6 27.7 %collective-permute-start.7 = (bf16[80,4096]{1,0:T(8,128)(2,1)}, bf16[80,4096]{1,0:T(8,128)(2,1)S(1)}, u32[]{:S(2)}, u32[]{:S(2)}) collective-permute-start(bf16[80,4096]{1,0:T(8,128)(2,1)} %get-tuple-element.14), channel_id=1, source_target_pairs={{0,64},{8,72},{16,80},{24,88},{32,96},{40,104},{48,112},{56,120},{... | collective-permute-start | bytes 1966088 | tf_op jit(solution)/shard_map/ppermute | solution.py:18
  515.3 28.9 %collective-permute-start.8 = (bf16[80,4096]{1,0:T(8,128)(2,1)}, bf16[80,4096]{1,0:T(8,128)(2,1)S(1)}, u32[]{:S(2)}, u32[]{:S(2)}) collective-permute-start(bf16[80,4096]{1,0:T(8,128)(2,1)} %get-tuple-element.13), channel_id=1, source_target_pairs={{0,72},{8,64},{16,88},{24,80},{32,104},{40,96},{48,120},{56,112},{... | collective-permute-start | bytes 1966088 | tf_op jit(solution)/shard_map/ppermute | solution.py:18
  529.3 29.1 %collective-permute-start.9 = (bf16[80,4096]{1,0:T(8,128)(2,1)}, bf16[80,4096]{1,0:T(8,128)(2,1)S(1)}, u32[]{:S(2)}, u32[]{:S(2)}) collective-permute-start(bf16[80,4096]{1,0:T(8,128)(2,1)} %get-tuple-element.12), channel_id=1, source_target_pairs={{0,80},{8,88},{16,64},{24,72},{32,112},{40,120},{48,96},{56,104},{... | collective-permute-start | bytes 1966088 | tf_op jit(solution)/shard_map/ppermute | solution.py:18
  544.2 28.1 %collective-permute-start.10 = (bf16[80,4096]{1,0:T(8,128)(2,1)S(1)}, bf16[80,4096]{1,0:T(8,128)(2,1)S(1)}, u32[]{:S(2)}, u32[]{:S(2)}) collective-permute-start(bf16[80,4096]{1,0:T(8,128)(2,1)S(1)} %copy-done.1), channel_id=1, source_target_pairs={{0,88},{8,80},{16,72},{24,64},{32,120},{40,112},{48,104},{56,96},{... | collective-permute-start | bytes 1966088 | tf_op jit(solution)/shard_map/ppermute | solution.py:18
  558.4 28.4 %collective-permute-start.11 = (bf16[80,4096]{1,0:T(8,128)(2,1)S(1)}, bf16[80,4096]{1,0:T(8,128)(2,1)S(1)}, u32[]{:S(2)}, u32[]{:S(2)}) collective-permute-start(bf16[80,4096]{1,0:T(8,128)(2,1)S(1)} %copy-done), channel_id=1, source_target_pairs={{0,96},{8,104},{16,112},{24,120},{32,64},{40,72},{48,80},{56,88},{... | collective-permute-start | bytes 1966088 | tf_op jit(solution)/shard_map/ppermute | solution.py:18
Sparse Core Ops, SparseCore 0:
  9.1 53.5 all-gather.1
  668.7 49.8 reduce-scatter.1
